TPU v7x, 32 devices: a whole 2x2x4 slice. The times are simulated.
32 devices in a mesh: rep: 2 (over x), sp: 16 (over z, y, core).
Axes of the slice: x: 2, y: 2, z: 4, core: 2. Of those that a mesh axis runs over, the one named last changes fastest.
Arguments:
- volume: bfloat16 [128, 16, 16, 128], P(('rep', 'sp')), parts along dimension 0, may hold values from -6 to 6
- first_kernel: bfloat16 [3, 3, 3, 128, 128], replicated, may hold values from -0.15625 to 0.15625
- second_kernel: bfloat16 [3, 3, 3, 128, 256], replicated, may hold values from -0.15625 to 0.15625
- deep_kernel: bfloat16 [3, 3, 3, 256, 512], P(None, None, None, None, 'sp'), may hold values from -0.109375 to 0.109375
- deeper_kernel: bfloat16 [3, 3, 3, 512, 512], P(None, None, None, None, 'sp'), may hold values from -0.078125 to 0.078125
- rise_kernel: bfloat16 [2, 2, 2, 512, 256], replicated, may hold values from -0.375 to 0.375
- decode_kernel: bfloat16 [3, 3, 3, 512, 256], P(None, None, None, 'sp'), may hold values from -0.078125 to 0.078125
- final_kernel: bfloat16 [2, 2, 2, 256, 128], replicated, may hold values from -0.5 to 0.5
Outputs:
- segmented: bfloat16 [128, 16, 16, 128], P(('rep', 'sp')), parts along dimension 0
There are 2 independent parts, one for each index of `rep`. A program takes and returns all parts, laid end to end along the dimension named above; an argument that names none is the same for every part. Nothing has to cross between parts.
All inputs are finite; a program needn't handle non-finite values.
Results may differ from a plain program's by a relative error of at most 0.015.
Values may be sent and summed in bfloat16 or wider, within the bound.
A program may use at most 64 MiB of HBM per device.

v0:
```python
import jax
import jax.numpy as jnp
from jax import lax
from jax.sharding import PartitionSpec as P


def with_halo(block, sides, width):
    for axis, dim in sides:
        count = lax.axis_size(axis)
        forward = [(i, i + 1) for i in range(count - 1)]
        backward = [(target, source) for source, target in forward]
        low = lax.ppermute(
            lax.slice_in_dim(block, block.shape[dim] - width, None, axis=dim), axis, forward
        )
        high = lax.ppermute(lax.slice_in_dim(block, 0, width, axis=dim), axis, backward)
        block = jnp.concatenate([low, block, high], axis=dim)
    return block


def conv_depth(padded, kernel):
    result = lax.conv_general_dilated(
        padded[None],
        kernel,
        (1, 1, 1),
        ((0, 0), (1, 1), (1, 1)),
        dimension_numbers=("NDHWC", "DHWIO", "NDHWC"),
        preferred_element_type=jnp.float32,
    )
    return result[0]


def pad_depth(values):
    return jnp.pad(values, ((1, 1), (0, 0), (0, 0), (0, 0)))


def pool_mean(values):
    depth, height, width, chans = values.shape
    blocks = values.astype(jnp.float32).reshape(depth // 2, 2, height // 2, 2, width // 2, 2, chans)
    return jnp.mean(blocks, axis=(1, 3, 5)).astype(jnp.bfloat16)


def up_conv(values, kernel):
    depth, height, width, chans = values.shape
    result = jnp.einsum("dhwi,abcio->dahbwco", values, kernel, preferred_element_type=jnp.float32)
    return result.reshape(2 * depth, 2 * height, 2 * width, kernel.shape[4])


def body(
    volume,
    first_kernel,
    second_kernel,
    deep_kernel,
    deeper_kernel,
    rise_kernel,
    decode_kernel,
    final_kernel,
):
    padded_input = with_halo(volume, (("sp", 0),), 1)
    first = jax.nn.relu(conv_depth(padded_input, first_kernel)).astype(jnp.bfloat16)
    pooled_one = pool_mean(first)
    padded_pool = with_halo(pooled_one, (("sp", 0),), 1)
    skip = jax.nn.relu(conv_depth(padded_pool, second_kernel)).astype(jnp.bfloat16)
    pooled_two = pool_mean(skip)
    pooled_whole = lax.all_gather(pooled_two, "sp", axis=0, tiled=True)
    deep_part = jax.nn.relu(conv_depth(pad_depth(pooled_whole), deep_kernel)).astype(jnp.bfloat16)
    deep_whole = lax.all_gather(deep_part, "sp", axis=3, tiled=True)
    deeper_part = jax.nn.relu(conv_depth(pad_depth(deep_whole), deeper_kernel)).astype(jnp.bfloat16)
    deeper_local = lax.all_to_all(deeper_part, "sp", split_axis=0, concat_axis=3, tiled=True)
    risen = up_conv(deeper_local, rise_kernel).astype(jnp.bfloat16)
    joined = jnp.concatenate([risen, skip], axis=3)
    padded_joined = with_halo(joined, (("sp", 0),), 1)
    whole_decode_kernel = lax.all_gather(decode_kernel, "sp", axis=3, tiled=True)
    decoded = jax.nn.relu(conv_depth(padded_joined, whole_decode_kernel)).astype(jnp.bfloat16)
    return up_conv(decoded, final_kernel).astype(jnp.bfloat16)


def solution(mesh):
    return jax.shard_map(
        body,
        mesh=mesh,
        in_specs=(
            P(("rep", "sp"), None, None, None),
            P(),
            P(),
            P(None, None, None, None, "sp"),
            P(None, None, None, None, "sp"),
            P(),
            P(None, None, None, "sp", None),
            P(),
        ),
        out_specs=P(("rep", "sp"), None, None, None),
        check_vma=False,
    )
```

profile of v0, /device:TPU:7, one launch (start us, length us, event | category | flops | bytes accessed | tf_op | source)
XLA Modules:
  0.0 139.4 jit_solution(17122065269597201188)
XLA Ops:
  6.5 0.7 all-gather.4.cloned.1.call-update
  7.3 1.0 copy.105
  8.3 0.0 copy-start.3
  8.3 0.0 copy-start.6
  8.3 3.8 %collective-permute-start = (bf16[1,16,16,128]{3,1,2,0:T(8,128)(2,1)S(1)}, bf16[1,16,16,128]{3,1,2,0:T(8,128)(2,1)S(1)}, u32[]{:S(2)}, u32[]{:S(2)}) collective-permute-start(bf16[1,16,16,128]{3,1,2,0:T(8,128)(2,1)S(1)} %get-tuple-element.5), channel_id=1, source_target_pairs={{0,1},{1,2},{2,3},{3,4},{4,5},{5,6},{6,7},{7,8},{8,9},{9,10},{10,1... | collective-permute-start | bytes 196616 | tf_op jit(solution)/shard_map/ppermute | solution.py:12
  12.2 1.9 %collective-permute-start.1 = (bf16[1,16,16,128]{3,1,2,0:T(8,128)(2,1)S(1)}, bf16[1,16,16,128]{3,1,2,0:T(8,128)(2,1)S(1)}, u32[]{:S(2)}, u32[]{:S(2)}) collective-permute-start(bf16[1,16,16,128]{3,1,2,0:T(8,128)(2,1)S(1)} %get-tuple-element.6), channel_id=1, source_target_pairs={{1,0},{2,1},{3,2},{4,3},{5,4},{6,5},{7,6},{8,7},{9,8},{10,9},{11,1... | collective-permute-start | bytes 196616 | tf_op jit(solution)/shard_map/ppermute | solution.py:15
  14.1 4.5 %collective-permute-done.1 = bf16[1,16,16,128]{3,1,2,0:T(8,128)(2,1)S(1)} collective-permute-done((bf16[1,16,16,128]{3,1,2,0:T(8,128)(2,1)S(1)}, bf16[1,16,16,128]{3,1,2,0:T(8,128)(2,1)S(1)}, u32[]{:S(2)}, u32[]{:S(2)}) %collective-permute-start.1) | collective-permute-done | bytes 65568 | tf_op jit(solution)/shard_map/ppermute | solution.py:15
  18.7 0.1 pad.10
  18.8 0.2 copy.109
  18.9 0.1 slice.28
  19.1 0.0 copy-start.2
  19.1 2.9 %fusion.4 = bf16[4,16,8,3,128]{4,2,3,1,0:T(8,128)(2,1)S(1)} fusion(bf16[3,3,3,128,128]{4,3,2,1,0:T(8,128)(2,1)S(1)} %copy-done.3, bf16[6,16,1,7,2,128]{5,3,4,1,0,2:T(8,128)(2,1)S(1)} %slice.28, bf16[6,16,1,8,3,128]{5,3,4,1,0,2:T(8,128)(2,1)S(1)} %copy.109, pred[8,3]{0,1:T(4,128)(4,1)S(1)} %copy-done.6), kind=kOutput, calls=%fused_computation.6 | convolution fusion | flops 1305870336 | bytes 2211864 | tf_op jit(solution)/shard_map/conv_general_dilated | solution.py:21
  22.0 0.1 copy.110
  22.1 0.3 convert_reduce_fusion
  22.4 1.9 %collective-permute-start.2 = (bf16[1,8,8,128]{3,1,2,0:T(8,128)(2,1)S(1)}, bf16[1,8,8,128]{3,1,2,0:T(8,128)(2,1)S(1)}, u32[]{:S(2)}, u32[]{:S(2)}) collective-permute-start(bf16[1,8,8,128]{3,1,2,0:T(8,128)(2,1)S(1)} %get-tuple-element.9), channel_id=1, source_target_pairs={{0,1},{1,2},{2,3},{3,4},{4,5},{5,6},{6,7},{7,8},{8,9},{9,10},{10,1... | collective-permute-start | bytes 49160 | tf_op jit(solution)/shard_map/ppermute | solution.py:12
  24.4 2.4 %collective-permute-start.3 = (bf16[1,8,8,128]{3,1,2,0:T(8,128)(2,1)S(1)}, bf16[1,8,8,128]{3,1,2,0:T(8,128)(2,1)S(1)}, u32[]{:S(2)}, u32[]{:S(2)}) collective-permute-start(bf16[1,8,8,128]{3,1,2,0:T(8,128)(2,1)S(1)} %get-tuple-element.10), channel_id=1, source_target_pairs={{1,0},{2,1},{3,2},{4,3},{5,4},{6,5},{7,6},{8,7},{9,8},{10,9},{11,1... | collective-permute-start | bytes 49160 | tf_op jit(solution)/shard_map/ppermute | solution.py:15
  26.8 4.7 %collective-permute-done.3 = bf16[1,8,8,128]{3,1,2,0:T(8,128)(2,1)S(1)} collective-permute-done((bf16[1,8,8,128]{3,1,2,0:T(8,128)(2,1)S(1)}, bf16[1,8,8,128]{3,1,2,0:T(8,128)(2,1)S(1)}, u32[]{:S(2)}, u32[]{:S(2)}) %collective-permute-start.3) | collective-permute-done | bytes 16416 | tf_op jit(solution)/shard_map/ppermute | solution.py:15
  31.5 0.0 copy-start.5
  31.5 1.5 %convert_reduce_fusion.1 = (f32[8,8,256]{2,1,0:T(8,128)S(1)}, bf16[1,2,8,8,256]{4,0,3,2,1:T(2,128)(2,1)S(1)}) fusion(bf16[3,3,3,128,256]{4,3,2,1,0:T(8,128)(2,1)S(1)} %copy-done.2, bf16[1,4,8,8,128]{4,2,3,1,0:T(8,128)(2,1)S(1)} %maximum_bitcast_fusion.2), kind=kOutput, calls=%fused_computation.39 | convolution fusion | flops 190431232 | bytes 1966080 | tf_op jit(solution)/shard_map/conv_general_dilated | solution.py:21
  33.0 0.1 reduce_sum.28
  33.1 16.9 %all-gather = bf16[64,4,256]{2,1,0:T(4,128)(2,1)S(1)} all-gather(bf16[4,4,256]{2,1,0:T(4,128)(2,1)S(1)} %multiply_convert_fusion.1), channel_id=2, replica_groups=mesh['rep'=2,'sp'=16] {'sp'}, dimensions={0}, use_global_device_ids=true | all-gather | bytes 139264 | tf_op jit(solution)/shard_map/all_gather | solution.py:64
  50.1 0.1 pad_bitcast_fusion.1
  50.1 2.9 %fusion.25 = bf16[1,16,4,4,32]{4,0,3,2,1:T(2,128)(2,1)S(1)} fusion(bf16[3,3,3,256,32]{3,4,2,1,0:T(8,128)(2,1)S(1)} %copy-done.5, bf16[1,18,4,4,256]{4,3,2,1,0:T(4,128)(2,1)S(1)} %pad_bitcast_fusion.1), kind=kOutput, calls=%fused_computation.28 | convolution fusion | flops 78643200 | bytes 606208 | tf_op jit(solution)/shard_map/conv_general_dilated | solution.py:21
  53.1 0.1 fusion.29
  53.1 0.2 copy.116
  53.3 37.2 %all-gather.1 = bf16[1,16,4,4,512]{1,3,2,0,4:T(4,128)(2,1)} all-gather(bf16[1,16,4,4,32]{1,3,2,0,4:T(4,128)(2,1)S(1)} %copy.116), channel_id=3, replica_groups=mesh['rep'=2,'sp'=16] {'sp'}, dimensions={4}, use_global_device_ids=true | all-gather | bytes 278528 | tf_op jit(solution)/shard_map/all_gather | solution.py:66
  90.5 2.8 %copy.117 = bf16[1,16,4,4,512]{4,1,3,2,0:T(8,128)(2,1)S(1)} copy(bf16[1,16,4,4,512]{1,3,2,0,4:T(4,128)(2,1)} %all-gather.1) | data formatting | bytes 524288 | tf_op jit(solution)/shard_map/all_gather | solution.py:66
  93.4 0.1 pad_bitcast_fusion
  93.5 5.8 %fusion.20 = bf16[1,16,4,4,32]{4,0,3,2,1:T(2,128)(2,1)S(1)} fusion(bf16[3,3,3,512,32]{3,4,2,1,0:T(8,128)(2,1)S(1)} %copy-done.4, bf16[1,18,4,4,512]{4,1,3,2,0:T(8,128)(2,1)S(1)} %pad_bitcast_fusion), kind=kOutput, calls=%fused_computation.20 | convolution fusion | flops 157286400 | bytes 1196032 | tf_op jit(solution)/shard_map/conv_general_dilated | solution.py:21
  99.3 0.1 fusion.30
  99.4 0.7 reshape.75
  100.1 6.0 %all-to-all-start = ((bf16[16,2,256]{2,1,0:T(2,128)(2,1)}), bf16[16,2,256]{2,1,0:T(2,128)(2,1)S(1)}, u32[]{:S(2)}, u32[]{:S(2)}) async-start(bf16[16,2,256]{2,1,0:T(2,128)(2,1)} %reshape.75), calls=%async_computation | async-start | bytes 32768 | tf_op jit(solution)/shard_map/all_to_all | solution.py:68
  106.1 0.1 copy.163
  106.2 4.9 %all-to-all-done = bf16[16,2,256]{2,1,0:T(2,128)(2,1)S(1)} async-done(((bf16[16,2,256]{2,1,0:T(2,128)(2,1)}), bf16[16,2,256]{2,1,0:T(2,128)(2,1)S(1)}, u32[]{:S(2)}, u32[]{:S(2)}) %all-to-all-start) | async-done | bytes 16416 | tf_op jit(solution)/shard_map/all_to_all | solution.py:68
  111.1 0.1 reshape.76
  111.2 0.1 reshape.69
  111.3 0.4 fusion.11
  111.8 0.1 copy.123
  111.8 0.3 slice_maximum_fusion
  112.1 3.4 %collective-permute-start.4 = (bf16[1,8,8,512]{3,0,2,1:T(2,128)(2,1)S(1)}, bf16[1,8,8,512]{3,0,2,1:T(2,128)(2,1)S(1)}, u32[]{:S(2)}, u32[]{:S(2)}) collective-permute-start(bf16[1,8,8,512]{3,0,2,1:T(2,128)(2,1)S(1)} %get-tuple-element.7), channel_id=1, source_target_pairs={{0,1},{1,2},{2,3},{3,4},{4,5},{5,6},{6,7},{7,8},{8,9},{9,10},{10,1... | collective-permute-start | bytes 196616 | tf_op jit(solution)/shard_map/ppermute | solution.py:12
  115.5 2.1 %collective-permute-start.5 = (bf16[1,8,8,512]{3,0,2,1:T(2,128)(2,1)S(1)}, bf16[1,8,8,512]{3,0,2,1:T(2,128)(2,1)S(1)}, u32[]{:S(2)}, u32[]{:S(2)}) collective-permute-start(bf16[1,8,8,512]{3,0,2,1:T(2,128)(2,1)S(1)} %get-tuple-element.8), channel_id=1, source_target_pairs={{1,0},{2,1},{3,2},{4,3},{5,4},{6,5},{7,6},{8,7},{9,8},{10,9},{11,1... | collective-permute-start | bytes 196616 | tf_op jit(solution)/shard_map/ppermute | solution.py:15
  117.6 5.0 %collective-permute-done.5 = bf16[1,8,8,512]{3,0,2,1:T(2,128)(2,1)S(1)} collective-permute-done((bf16[1,8,8,512]{3,0,2,1:T(2,128)(2,1)S(1)}, bf16[1,8,8,512]{3,0,2,1:T(2,128)(2,1)S(1)}, u32[]{:S(2)}, u32[]{:S(2)}) %collective-permute-start.5) | collective-permute-done | bytes 65568 | tf_op jit(solution)/shard_map/ppermute | solution.py:15
  122.7 0.4 maximum_bitcast_fusion.1
  123.1 0.0 copy-start.1
  123.1 0.0 all-gather.4.cloned.1.call-done
  123.1 8.2 %fusion.6 = bf16[1,2,8,8,256]{4,0,3,2,1:T(2,128)(2,1)S(1)} fusion(bf16[3,3,3,512,256]{4,3,2,1,0:T(8,128)(2,1)} %all-gather.4.cloned.1.call-done, bf16[1,4,8,8,512]{4,1,3,2,0:T(4,128)(2,1)S(1)} %maximum_bitcast_fusion.1), kind=kOutput, calls=%fused_computation.10 | convolution fusion | flops 761331712 | bytes 7405568 | tf_op jit(solution)/shard_map/conv_general_dilated | solution.py:21
  131.3 0.2 fusion.5
  131.6 0.9 copy.127
  (23 shorter events, 0.2 us)
Async XLA Ops:
  6.5 104.8 %copy-start = (bf16[2,2,2,512,256]{4,3,2,1,0:T(8,128)(2,1)S(1)}, bf16[2,2,2,512,256]{4,3,2,1,0:T(8,128)(2,1)}, u32[]{:S(2)}) copy-start(bf16[2,2,2,512,256]{4,3,2,1,0:T(8,128)(2,1)} %param.13) | copy-start | bytes 6291460
  6.5 116.6 %all-gather.4.cloned.1.call-start = ((), (), s32[]{:S(2)}) async-start(), calls=%async_computation.1 | async-start | bytes 7520256 | tf_op jit(solution)/shard_map/all_gather | solution.py:72
  8.3 10.8 %copy-start.3 = (bf16[3,3,3,128,128]{4,3,2,1,0:T(8,128)(2,1)S(1)}, bf16[3,3,3,128,128]{4,3,2,1,0:T(8,128)(2,1)}, u32[]{:S(2)}) copy-start(bf16[3,3,3,128,128]{4,3,2,1,0:T(8,128)(2,1)} %param.9) | copy-start | bytes 2654212
  8.3 10.8 %copy-start.6 = (pred[8,3]{0,1:T(4,128)(4,1)S(1)}, pred[8,3]{0,1:T(4,128)(4,1)}, u32[]{:S(2)}) copy-start(pred[8,3]{0,1:T(4,128)(4,1)} %constant.27) | copy-start | bytes 76
  8.3 5.8 %collective-permute-start = (bf16[1,16,16,128]{3,1,2,0:T(8,128)(2,1)S(1)}, bf16[1,16,16,128]{3,1,2,0:T(8,128)(2,1)S(1)}, u32[]{:S(2)}, u32[]{:S(2)}) collective-permute-start(bf16[1,16,16,128]{3,1,2,0:T(8,128)(2,1)S(1)} %get-tuple-element.5), channel_id=1, source_target_pairs={{0,1},{1,2},{2,3},{3,4},{4,5},{5,6},{6,7},{7,8},{8,9},{9,10},{10,1... | collective-permute-start | bytes 196616 | tf_op jit(solution)/shard_map/ppermute | solution.py:12
  12.2 6.5 %collective-permute-start.1 = (bf16[1,16,16,128]{3,1,2,0:T(8,128)(2,1)S(1)}, bf16[1,16,16,128]{3,1,2,0:T(8,128)(2,1)S(1)}, u32[]{:S(2)}, u32[]{:S(2)}) collective-permute-start(bf16[1,16,16,128]{3,1,2,0:T(8,128)(2,1)S(1)} %get-tuple-element.6), channel_id=1, source_target_pairs={{1,0},{2,1},{3,2},{4,3},{5,4},{6,5},{7,6},{8,7},{9,8},{10,9},{11,1... | collective-permute-start | bytes 196616 | tf_op jit(solution)/shard_map/ppermute | solution.py:15
  19.1 12.4 %copy-start.2 = (bf16[3,3,3,128,256]{4,3,2,1,0:T(8,128)(2,1)S(1)}, bf16[3,3,3,128,256]{4,3,2,1,0:T(8,128)(2,1)}, u32[]{:S(2)}) copy-start(bf16[3,3,3,128,256]{4,3,2,1,0:T(8,128)(2,1)} %param.10) | copy-start | bytes 5308420
  22.4 4.3 %collective-permute-start.2 = (bf16[1,8,8,128]{3,1,2,0:T(8,128)(2,1)S(1)}, bf16[1,8,8,128]{3,1,2,0:T(8,128)(2,1)S(1)}, u32[]{:S(2)}, u32[]{:S(2)}) collective-permute-start(bf16[1,8,8,128]{3,1,2,0:T(8,128)(2,1)S(1)} %get-tuple-element.9), channel_id=1, source_target_pairs={{0,1},{1,2},{2,3},{3,4},{4,5},{5,6},{6,7},{7,8},{8,9},{9,10},{10,1... | collective-permute-start | bytes 49160 | tf_op jit(solution)/shard_map/ppermute | solution.py:12
  24.4 7.1 %collective-permute-start.3 = (bf16[1,8,8,128]{3,1,2,0:T(8,128)(2,1)S(1)}, bf16[1,8,8,128]{3,1,2,0:T(8,128)(2,1)S(1)}, u32[]{:S(2)}, u32[]{:S(2)}) collective-permute-start(bf16[1,8,8,128]{3,1,2,0:T(8,128)(2,1)S(1)} %get-tuple-element.10), channel_id=1, source_target_pairs={{1,0},{2,1},{3,2},{4,3},{5,4},{6,5},{7,6},{8,7},{9,8},{10,9},{11,1... | collective-permute-start | bytes 49160 | tf_op jit(solution)/shard_map/ppermute | solution.py:15
  31.5 18.6 %copy-start.5 = (bf16[3,3,3,256,32]{3,4,2,1,0:T(8,128)(2,1)S(1)}, bf16[3,3,3,256,32]{3,4,2,1,0:T(8,128)(2,1)}, u32[]{:S(2)}) copy-start(bf16[3,3,3,256,32]{3,4,2,1,0:T(8,128)(2,1)} %param.11) | copy-start | bytes 1327108
  53.3 40.2 %copy-start.4 = (bf16[3,3,3,512,32]{3,4,2,1,0:T(8,128)(2,1)S(1)}, bf16[3,3,3,512,32]{3,4,2,1,0:T(8,128)(2,1)}, u32[]{:S(2)}) copy-start(bf16[3,3,3,512,32]{3,4,2,1,0:T(8,128)(2,1)} %param.12) | copy-start | bytes 2654212
  100.1 11.0 %all-to-all-start = ((bf16[16,2,256]{2,1,0:T(2,128)(2,1)}), bf16[16,2,256]{2,1,0:T(2,128)(2,1)S(1)}, u32[]{:S(2)}, u32[]{:S(2)}) async-start(bf16[16,2,256]{2,1,0:T(2,128)(2,1)} %reshape.75), calls=%async_computation | async-start | bytes 32768 | tf_op jit(solution)/shard_map/all_to_all | solution.py:68
  112.1 5.5 %collective-permute-start.4 = (bf16[1,8,8,512]{3,0,2,1:T(2,128)(2,1)S(1)}, bf16[1,8,8,512]{3,0,2,1:T(2,128)(2,1)S(1)}, u32[]{:S(2)}, u32[]{:S(2)}) collective-permute-start(bf16[1,8,8,512]{3,0,2,1:T(2,128)(2,1)S(1)} %get-tuple-element.7), channel_id=1, source_target_pairs={{0,1},{1,2},{2,3},{3,4},{4,5},{5,6},{6,7},{7,8},{8,9},{9,10},{10,1... | collective-permute-start | bytes 196616 | tf_op jit(solution)/shard_map/ppermute | solution.py:12
  115.5 7.2 %collective-permute-start.5 = (bf16[1,8,8,512]{3,0,2,1:T(2,128)(2,1)S(1)}, bf16[1,8,8,512]{3,0,2,1:T(2,128)(2,1)S(1)}, u32[]{:S(2)}, u32[]{:S(2)}) collective-permute-start(bf16[1,8,8,512]{3,0,2,1:T(2,128)(2,1)S(1)} %get-tuple-element.8), channel_id=1, source_target_pairs={{1,0},{2,1},{3,2},{4,3},{5,4},{6,5},{7,6},{8,7},{9,8},{10,9},{11,1... | collective-permute-start | bytes 196616 | tf_op jit(solution)/shard_map/ppermute | solution.py:15
  123.1 8.2 %copy-start.1 = (bf16[2,2,2,256,128]{4,3,2,1,0:T(8,128)(2,1)S(1)}, bf16[2,2,2,256,128]{4,3,2,1,0:T(8,128)(2,1)}, u32[]{:S(2)}) copy-start(bf16[2,2,2,256,128]{4,3,2,1,0:T(8,128)(2,1)} %param.15) | copy-start | bytes 1572868
Sparse Core Ops, SparseCore 0:
  9.5 82.1 all-gather.3
where the time goes:
time: 140 us; the launch traced here: 139 us
  blocking collectives  54.1 us (39%)
  matrix products  21.9 us (16%)
  starting transfers between devices  21.6 us (15%)
  waiting for transfers between devices  19.9 us (14%)
  between operations  13.8 us (10%)
  local copies, waits for them, and re-layouts  6.71 us (5%)
    all_gather x1, blocking collectives, body(): deep_whole = lax.all_gather(deep_part, 'sp', axis=3, tiled=True)  37.2 us
    conv_general_dilated x5, matrix products, conv_depth(): lax.conv_general_dilated(padded[None], kernel, (1, 1, 1), ((0, 0), (1, 1)...  21.3 us
    all_gather x1, blocking collectives, body(): pooled_whole = lax.all_gather(pooled_two, 'sp', axis=0, tiled=True)  16.9 us
    ppermute x3, waiting for transfers between devices, with_halo(): lax.ppermute(lax.slice_in_dim(block, 0, width, axis=dim), axis, backward)  14.3 us
    ppermute x3, starting transfers between devices, with_halo(): lax.ppermute(lax.slice_in_dim(block, block.shape[dim] - width, None, axis...  9.13 us
    ppermute x3, starting transfers between devices, with_halo(): lax.ppermute(lax.slice_in_dim(block, 0, width, axis=dim), axis, backward)  6.47 us
    all_to_all x1, starting transfers between devices, body(): lax.all_to_all(deeper_part, 'sp', split_axis=0, concat_axis=3, tiled=True)  5.96 us
    all_to_all x1, waiting for transfers between devices, body(): lax.all_to_all(deeper_part, 'sp', split_axis=0, concat_axis=3, tiled=True)  4.92 us
  transfers between devices with their start and end apart: 8, of which 4 were waited for; matrix products, arithmetic and copies ran while one was open for 15% of the time, Pallas kernels for 0%

commit v1 on v0

v1 whole, which is shorter than its diff:
```python
import functools

import jax
import jax.numpy as jnp
from jax import lax
from jax.experimental import pallas as pl
from jax.experimental.pallas import tpu as pltpu
from jax.sharding import PartitionSpec as P

LANES = 128


def halo_slices(block, axis):
    count = lax.axis_size(axis)
    forward = [(i, i + 1) for i in range(count - 1)]
    backward = [(target, source) for source, target in forward]
    low = lax.ppermute(block[-1:], axis, forward)
    high = lax.ppermute(block[:1], axis, backward)
    return low, high


def with_halo(block, axis):
    low, high = halo_slices(block, axis)
    return jnp.concatenate([low, block, high], axis=0)


def conv_depth(padded, kernel):
    result = lax.conv_general_dilated(
        padded[None],
        kernel,
        (1, 1, 1),
        ((0, 0), (1, 1), (1, 1)),
        dimension_numbers=("NDHWC", "DHWIO", "NDHWC"),
        preferred_element_type=jnp.float32,
    )
    return result[0]


def pool_mean(values):
    depth, height, width, chans = values.shape
    blocks = values.astype(jnp.float32).reshape(depth // 2, 2, height // 2, 2, width // 2, 2, chans)
    return jnp.mean(blocks, axis=(1, 3, 5)).astype(jnp.bfloat16)


def up_conv(values, kernel):
    depth, height, width, chans = values.shape
    result = jnp.einsum("dhwi,abcio->dahbwco", values, kernel, preferred_element_type=jnp.float32)
    return result.reshape(2 * depth, 2 * height, 2 * width, kernel.shape[4])


def conv_rows(values, weight_ref, height, width):
    rows = values.shape[0]
    index = lax.broadcasted_iota(jnp.int32, (rows, 1), 0)
    w_at = index & (width - 1)
    h_at = (index >> (width.bit_length() - 1)) & (height - 1)
    total = jnp.zeros((rows, LANES), jnp.float32)
    for b in range(3):
        for c in range(3):
            shift = width * (b - 1) + (c - 1)
            moved = values if shift == 0 else pltpu.roll(values, (-shift) % rows, 0)
            h_to, w_to = h_at + (b - 1), w_at + (c - 1)
            keep = (h_to >= 0) & (h_to < height) & (w_to >= 0) & (w_to < width)
            moved = jnp.where(keep, moved, 0.0).astype(jnp.bfloat16)
            total += jnp.dot(moved, weight_ref[3 * b + c], preferred_element_type=jnp.float32)
    return total


def bottleneck_kernel(
    n, height, width, part,
    pooled_ref, deep_w_ref, deeper_w_ref, out_ref,
    whole, deep_mine, deep_all, packed,
    send_a, recv_a, send_b, recv_b, send_c, recv_c,
):
    me = lax.axis_index("sp")
    area = height * width
    voxels = n * area
    partner = me + 1 - 2 * (me % 2)
    half = n // 2

    barrier = pltpu.get_barrier_semaphore()

    def greet(k, carry):
        pl.semaphore_signal(
            barrier, inc=1, device_id={"sp": lax.rem(me + k, n)},
            device_id_type=pl.DeviceIdType.MESH,
        )
        return carry

    lax.fori_loop(1, n, greet, 0)
    pl.semaphore_wait(barrier, n - 1)

    def copy_to(src, dst, send_sem, recv_sem, target):
        return pltpu.make_async_remote_copy(
            src_ref=src, dst_ref=dst, send_sem=send_sem, recv_sem=recv_sem,
            device_id={"sp": target}, device_id_type=pl.DeviceIdType.MESH,
        )

    def gather(mine, everyone, send_sem, recv_sem):
        def slot(source):
            return everyone.at[source]

        def direct(k):
            target = lax.rem(me + 2 * k, n)
            return copy_to(mine, slot(me), send_sem.at[k], recv_sem.at[me], target)

        def relay(k):
            source = lax.rem(me + 2 * (half - k), n)
            return copy_to(
                slot(source), slot(source), send_sem.at[half + k], recv_sem.at[source], partner
            )

        def arrival(source):
            return copy_to(mine, slot(source), send_sem.at[0], recv_sem.at[source], partner)

        def start_direct(k, carry):
            direct(k).start()
            return carry

        to_partner = copy_to(mine, slot(me), send_sem.at[0], recv_sem.at[me], partner)
        lax.fori_loop(1, half, start_direct, 0)
        to_partner.start()
        everyone[me] = mine[...]

        def pass_on(k, carry):
            arrival(lax.rem(me + 2 * (half - k), n)).wait_recv()
            relay(k).start()
            return carry

        lax.fori_loop(1, half, pass_on, 0)

        def from_partner(k, carry):
            arrival(lax.rem(partner + 2 * (half - k), n)).wait_recv()
            return carry

        lax.fori_loop(0, half, from_partner, 0)

        def finish():
            to_partner.wait_send()

            def sent(k, carry):
                direct(k).wait_send()
                relay(k).wait_send()
                return carry

            lax.fori_loop(1, half, sent, 0)

        return finish

    finish_a = gather(pooled_ref, whole, send_a, recv_a)
    lanes = lax.broadcasted_iota(jnp.int32, (1, voxels), 1)
    values = whole[...].astype(jnp.float32).reshape(voxels, pooled_ref.shape[1])
    deep = conv_rows(values, deep_w_ref, height, width).T
    below = jnp.where(lanes >= area, pltpu.roll(deep[0:part], area, 1), 0.0)
    above = jnp.where(
        lanes < voxels - area, pltpu.roll(deep[2 * part : 3 * part], voxels - area, 1), 0.0
    )
    deep = below + deep[part : 2 * part] + above
    deep_mine[...] = jnp.maximum(deep, 0.0).astype(jnp.bfloat16)
    finish_b = gather(deep_mine, deep_all, send_b, recv_b)

    values = deep_all[...].astype(jnp.float32).reshape(n * part, voxels).T
    deeper = conv_rows(values, deeper_w_ref, height, width)
    rows = lax.broadcasted_iota(jnp.int32, (voxels, 1), 0)

    def down(block):
        return jnp.where(rows >= area, pltpu.roll(block, area, 0), 0.0)

    def up(block):
        return jnp.where(rows < voxels - area, pltpu.roll(block, voxels - area, 0), 0.0)

    deeper = (
        down(deeper)
        + pltpu.roll(deeper, LANES - part, 1)
        + up(pltpu.roll(deeper, LANES - 2 * part, 1))
    )
    deeper = jnp.maximum(deeper, 0.0)
    lane = lax.broadcasted_iota(jnp.int32, (1, LANES), 1)
    deeper = jnp.where(
        lane < part,
        down(deeper),
        jnp.where(
            lane < 2 * part,
            pltpu.roll(deeper, part, 1),
            up(pltpu.roll(deeper, 2 * part, 1)),
        ),
    )
    packed[...] = deeper.astype(jnp.bfloat16).reshape(n, area, LANES)

    def deal(k):
        target = lax.rem(me + k, n)
        return copy_to(packed.at[target], out_ref.at[me], send_c.at[k], recv_c.at[me], target)

    def start_deal(k, carry):
        deal(k).start()
        return carry

    lax.fori_loop(1, n, start_deal, 0)
    out_ref[me] = packed[me]

    def receive(k, carry):
        source = lax.rem(me + k, n)
        copy_to(
            packed.at[source], out_ref.at[source], send_c.at[k], recv_c.at[source], source
        ).wait_recv()
        return carry

    lax.fori_loop(1, n, receive, 0)

    def sent(k, carry):
        deal(k).wait_send()
        return carry

    lax.fori_loop(1, n, sent, 0)
    finish_a()
    finish_b()


def stack_taps(kernel):
    chans, part = kernel.shape[3], kernel.shape[4]
    stacked = jnp.transpose(kernel, (1, 2, 3, 0, 4)).reshape(9, chans, 3 * part)
    return jnp.pad(stacked, ((0, 0), (0, 0), (0, LANES - 3 * part)))


def bottleneck(pooled, deep_kernel, deeper_kernel):
    n = lax.axis_size("sp")
    _, height, width, chans = pooled.shape
    part = deep_kernel.shape[4]
    area = height * width
    voxels = n * area
    vmem = pl.BlockSpec(memory_space=pltpu.VMEM)
    received = pl.pallas_call(
        functools.partial(bottleneck_kernel, n, height, width, part),
        out_shape=jax.ShapeDtypeStruct((n, area, LANES), jnp.bfloat16),
        in_specs=[vmem] * 3,
        out_specs=vmem,
        scratch_shapes=[
            pltpu.VMEM((n, area, chans), jnp.bfloat16),
            pltpu.VMEM((part, voxels), jnp.bfloat16),
            pltpu.VMEM((n, part, voxels), jnp.bfloat16),
            pltpu.VMEM((n, area, LANES), jnp.bfloat16),
        ]
        + [pltpu.SemaphoreType.DMA((n,))] * 6,
        compiler_params=pltpu.CompilerParams(collective_id=0, has_side_effects=True),
        name="bottleneck",
    )(pooled.reshape(area, chans), stack_taps(deep_kernel), stack_taps(deeper_kernel))
    blocks = received[:, :, : 3 * part].reshape(n, area, 3, part)
    return jnp.transpose(blocks, (2, 1, 0, 3)).reshape(3, height, width, n * part)


def body(
    volume,
    first_kernel,
    second_kernel,
    deep_kernel,
    deeper_kernel,
    rise_kernel,
    decode_kernel,
    final_kernel,
):
    padded_input = with_halo(volume, "sp")
    first = jax.nn.relu(conv_depth(padded_input, first_kernel)).astype(jnp.bfloat16)
    pooled_one = pool_mean(first)
    padded_pool = with_halo(pooled_one, "sp")
    skip = jax.nn.relu(conv_depth(padded_pool, second_kernel)).astype(jnp.bfloat16)
    pooled_two = pool_mean(skip)
    padded_skip = with_halo(skip, "sp")
    deeper_near = bottleneck(pooled_two, deep_kernel, deeper_kernel)
    risen = up_conv(deeper_near, rise_kernel)[1:-1].astype(jnp.bfloat16)
    padded_joined = jnp.concatenate([risen, padded_skip], axis=3)
    whole_decode_kernel = lax.all_gather(decode_kernel, "sp", axis=3, tiled=True)
    decoded = jax.nn.relu(conv_depth(padded_joined, whole_decode_kernel)).astype(jnp.bfloat16)
    return up_conv(decoded, final_kernel).astype(jnp.bfloat16)


def solution(mesh):
    return jax.shard_map(
        body,
        mesh=mesh,
        in_specs=(
            P(("rep", "sp"), None, None, None),
            P(),
            P(),
            P(None, None, None, None, "sp"),
            P(None, None, None, None, "sp"),
            P(),
            P(None, None, None, "sp", None),
            P(),
        ),
        out_specs=P(("rep", "sp"), None, None, None),
        check_vma=False,
    )
```

time: 140 us -> 99.6 us (0.71)
  the two profiles are of different devices: /device:TPU:7 before, /device:TPU:0 now
where the time goes in v1:
time: 99.6 us; the launch traced here: 99.1 us
  Pallas kernels  33.5 us (34%)
  matrix products  16.9 us (17%)
  starting transfers between devices  14.4 us (14%)
  between operations  13.7 us (14%)
  local copies, waits for them, and re-layouts  13.1 us (13%)
  waiting for transfers between devices  4.7 us (5%)
  other arithmetic  2.88 us (3%)
    pallas_call x1, Pallas kernels, bottleneck(): pl.pallas_call(functools.partial(bottleneck_kernel, n, height, width, par...  33.5 us
    conv_general_dilated x3, matrix products, conv_depth(): lax.conv_general_dilated(padded[None], kernel, (1, 1, 1), ((0, 0), (1, 1)...  16.2 us
    ppermute x3, starting transfers between devices, halo_slices(): low = lax.ppermute(block[-1:], axis, forward)  10.4 us
    ppermute x3, starting transfers between devices, halo_slices(): high = lax.ppermute(block[:1], axis, backward)  4.06 us
    ppermute x3, waiting for transfers between devices, halo_slices(): high = lax.ppermute(block[:1], axis, backward)  3.96 us
    reshape x2, local copies, waits for them, and re-layouts, stack_taps(): stacked = jnp.transpose(kernel, (1, 2, 3, 0, 4)).reshape(9, chans, 3 * part)  3.77 us
    unnamed x15, local copies, waits for them, and re-layouts  2.85 us
    pad x2, local copies, waits for them, and re-layouts, stack_taps(): return jnp.pad(stacked, ((0, 0), (0, 0), (0, LANES - 3 * part)))  2.28 us
  transfers between devices with their start and end apart: 7, of which 1 were waited for; matrix products, arithmetic and copies ran while one was open for 24% of the time, Pallas kernels for 34%

profile of v1, /device:TPU:0, one launch (start us, length us, event | category | flops | bytes accessed | tf_op | source)
XLA Modules:
  0.0 99.1 jit_solution(13056317419417564789)
XLA Ops:
  6.5 0.0 copy-start
  6.5 0.0 all-gather.2.cloned.1.call-start
  6.5 0.7 all-gather.2.cloned.1.call-update
  7.3 0.9 fusion.20
  8.1 2.4 %collective-permute-start = (bf16[1,16,16,128]{3,2,1,0:T(8,128)(2,1)S(1)}, bf16[1,16,16,128]{3,2,1,0:T(8,128)(2,1)S(1)}, u32[]{:S(2)}, u32[]{:S(2)}) collective-permute-start(bf16[1,16,16,128]{3,2,1,0:T(8,128)(2,1)S(1)} %get-tuple-element.5), channel_id=1, source_target_pairs={{0,1},{1,2},{2,3},{3,4},{4,5},{5,6},{6,7},{7,8},{8,9},{9,10},{10,1... | collective-permute-start | bytes 196616 | tf_op jit(solution)/shard_map/ppermute | solution.py:17
  10.6 1.3 %collective-permute-start.1 = (bf16[1,16,16,128]{3,2,1,0:T(8,128)(2,1)S(1)}, bf16[1,16,16,128]{3,2,1,0:T(8,128)(2,1)S(1)}, u32[]{:S(2)}, u32[]{:S(2)}) collective-permute-start(bf16[1,16,16,128]{3,2,1,0:T(8,128)(2,1)S(1)} %get-tuple-element.6), channel_id=1, source_target_pairs={{1,0},{2,1},{3,2},{4,3},{5,4},{6,5},{7,6},{8,7},{9,8},{10,9},{11,1... | collective-permute-start | bytes 196616 | tf_op jit(solution)/shard_map/ppermute | solution.py:18
  11.9 0.0 collective-permute-done
  11.9 4.0 %collective-permute-done.1 = bf16[1,16,16,128]{3,2,1,0:T(8,128)(2,1)S(1)} collective-permute-done((bf16[1,16,16,128]{3,2,1,0:T(8,128)(2,1)S(1)}, bf16[1,16,16,128]{3,2,1,0:T(8,128)(2,1)S(1)}, u32[]{:S(2)}, u32[]{:S(2)}) %collective-permute-start.1) | collective-permute-done | bytes 65568 | tf_op jit(solution)/shard_map/ppermute | solution.py:18
  15.8 1.0 %maximum_bitcast_fusion = bf16[1,6,16,16,128]{4,3,2,1,0:T(8,128)(2,1)S(1)} fusion(bf16[1,16,16,128]{3,2,1,0:T(8,128)(2,1)S(1)} %collective-permute-done.1, bf16[4,16,16,128]{3,2,1,0:T(8,128)(2,1)} %param.8, bf16[1,16,16,128]{3,2,1,0:T(8,128)(2,1)S(1)} %collective-permute-done), kind=kLoop, calls=%fused_computation.16 | loop fusion | flops 393216 | bytes 786432 | tf_op jit(solution)/shard_map/broadcast_in_dim | solution.py:29
  16.8 0.0 copy-start.2
  16.8 6.6 %fusion.3 = f32[1,4,16,16,128]{4,0,3,2,1:T(1,128)S(1)} fusion(bf16[3,3,3,128,128]{4,3,2,1,0:T(8,128)(2,1)} %param.9, bf16[1,6,16,16,128]{4,3,2,1,0:T(8,128)(2,1)S(1)} %maximum_bitcast_fusion), kind=kOutput, calls=%fused_computation.4 | convolution fusion | flops 832438272 | bytes 1802240 | tf_op jit(solution)/shard_map/conv_general_dilated | solution.py:28
  23.4 0.9 reduce_sum.21
  24.4 0.8 multiply_convert_fusion
  25.2 4.9 %collective-permute-start.2 = (bf16[1,8,8,128]{3,2,1,0:T(8,128)(2,1)S(1)}, bf16[1,8,8,128]{3,2,1,0:T(8,128)(2,1)S(1)}, u32[]{:S(2)}, u32[]{:S(2)}) collective-permute-start(bf16[1,8,8,128]{3,2,1,0:T(8,128)(2,1)S(1)} %get-tuple-element.9), channel_id=1, source_target_pairs={{0,1},{1,2},{2,3},{3,4},{4,5},{5,6},{6,7},{7,8},{8,9},{9,10},{10,1... | collective-permute-start | bytes 49160 | tf_op jit(solution)/shard_map/ppermute | solution.py:17
  30.2 1.3 %collective-permute-start.3 = (bf16[1,8,8,128]{3,2,1,0:T(8,128)(2,1)S(1)}, bf16[1,8,8,128]{3,2,1,0:T(8,128)(2,1)S(1)}, u32[]{:S(2)}, u32[]{:S(2)}) collective-permute-start(bf16[1,8,8,128]{3,2,1,0:T(8,128)(2,1)S(1)} %get-tuple-element.10), channel_id=1, source_target_pairs={{1,0},{2,1},{3,2},{4,3},{5,4},{6,5},{7,6},{8,7},{9,8},{10,9},{11,1... | collective-permute-start | bytes 49160 | tf_op jit(solution)/shard_map/ppermute | solution.py:18
  31.5 0.0 copy-done.2
  31.5 1.0 copy.48
  32.4 1.6 %copy.49 = bf16[9,512,96]{2,1,0:T(8,128)(2,1)S(1)} copy(bf16[9,512,96]{1,2,0:T(8,128)(2,1)} %bitcast.56) | data formatting | bytes 1769472 | tf_op jit(solution)/shard_map/reshape | solution.py:220
  34.1 1.8 %copy.46 = bf16[3,3,3,256,32]{3,4,0,2,1:T(8,128)(2,1)} copy(bf16[3,3,3,256,32]{3,4,2,1,0:T(8,128)(2,1)} %param.11) | data formatting | bytes 884736 | tf_op args[3]
  35.9 2.1 %copy.47 = bf16[9,256,96]{2,1,0:T(8,128)(2,1)} copy(bf16[9,256,96]{1,2,0:T(8,128)(2,1)} %bitcast.57) | data formatting | bytes 884736 | tf_op jit(solution)/shard_map/reshape | solution.py:220
  38.0 1.3 %pad.9.deeper_w_ref = bf16[9,512,128]{2,1,0:T(8,128)(2,1)} pad(bf16[9,512,96]{2,1,0:T(8,128)(2,1)S(1)} %copy.49, bf16[]{:T(256)} %constant.14.clone.1), padding=0_0x0_0x0_32 | pad | bytes 2064386 | tf_op jit(solution)/shard_map/jit(_pad)/pad | solution.py:221
  39.3 0.0 copy-done.1
  39.3 1.0 %pad.8.deep_w_ref = bf16[9,256,128]{2,1,0:T(8,128)(2,1)} pad(bf16[9,256,96]{2,1,0:T(8,128)(2,1)S(1)} %copy-done.1, bf16[]{:T(256)} %constant.14.clone.1), padding=0_0x0_0x0_32 | pad | bytes 1032194 | tf_op jit(solution)/shard_map/jit(_pad)/pad | solution.py:221
  40.3 0.0 collective-permute-done.2
  40.3 0.0 collective-permute-done.3
  40.4 0.0 copy-done.4
  40.4 1.5 %convert_reduce_fusion = (f32[8,8,256]{2,1,0:T(8,128)S(1)}, bf16[1,2,8,8,256]{4,0,3,2,1:T(2,128)(2,1)S(1)}) fusion(bf16[3,3,3,128,256]{4,3,2,1,0:T(8,128)(2,1)S(1)} %copy-done.4, bf16[1,4,8,8,128]{4,3,2,1,0:T(8,128)(2,1)S(1)} %maximum_bitcast_fusion.2), kind=kOutput, calls=%fused_computation.19 | convolution fusion | flops 190431232 | bytes 1966080 | tf_op jit(solution)/shard_map/conv_general_dilated | solution.py:28
  41.9 0.1 fusion.21
  42.0 3.0 %collective-permute-start.4 = (bf16[1,8,8,256]{3,2,1,0:T(8,128)(2,1)S(1)}, bf16[1,8,8,256]{3,2,1,0:T(8,128)(2,1)S(1)}, u32[]{:S(2)}, u32[]{:S(2)}) collective-permute-start(bf16[1,8,8,256]{3,2,1,0:T(8,128)(2,1)S(1)} %bitcast.62), channel_id=1, source_target_pairs={{0,1},{1,2},{2,3},{3,4},{4,5},{5,6},{6,7},{7,8},{8,9},{9,10},{10,1... | collective-permute-start | bytes 98312 | tf_op jit(solution)/shard_map/ppermute | solution.py:17
  45.1 1.5 %collective-permute-start.5 = (bf16[1,8,8,256]{3,2,1,0:T(8,128)(2,1)S(1)}, bf16[1,8,8,256]{3,2,1,0:T(8,128)(2,1)S(1)}, u32[]{:S(2)}, u32[]{:S(2)}) collective-permute-start(bf16[1,8,8,256]{3,2,1,0:T(8,128)(2,1)S(1)} %bitcast.63), channel_id=1, source_target_pairs={{1,0},{2,1},{3,2},{4,3},{5,4},{6,5},{7,6},{8,7},{9,8},{10,9},{11,1... | collective-permute-start | bytes 98312 | tf_op jit(solution)/shard_map/ppermute | solution.py:18
  46.6 0.1 reduce_sum.28
  46.7 0.6 convert_element_type.72.pooled_ref
  47.3 33.5 %bottleneck.1 = bf16[16,16,128]{2,1,0:T(8,128)(2,1)} custom-call(bf16[16,256]{1,0:T(8,128)(2,1)} %convert_element_type.72.pooled_ref, bf16[9,256,128]{2,1,0:T(8,128)(2,1)} %pad.8.deep_w_ref, bf16[9,512,128]{2,1,0:T(8,128)(2,1)} %pad.9.deeper_w_ref), custom_call_target="tpu_custom_call" | custom-call | tf_op jit(solution)/shard_map/bottleneck/pallas_call | solution.py:231
  80.8 1.0 reshape.50
  81.8 0.2 copy.50
  81.9 0.2 reshape.54
  82.1 0.0 copy-done
  82.1 0.5 fusion.8
  82.6 0.2 copy.51
  82.8 0.1 reshape.52
  82.9 0.0 collective-permute-done.4
  82.9 0.0 collective-permute-done.5
  82.9 0.0 copy-start.3
  83.0 0.0 all-gather.2.cloned.1.call-done
  83.0 8.1 %fusion.11 = bf16[1,2,8,8,256]{4,0,3,2,1:T(2,128)(2,1)S(1)} fusion(bf16[3,3,3,512,256]{4,3,2,1,0:T(8,128)(2,1)} %all-gather.2.cloned.1.call-done, bf16[1,4,8,8,512]{4,3,2,1,0:T(8,128)(2,1)S(1)} %maximum_bitcast_fusion.1), kind=kOutput, calls=%fused_computation.10 | convolution fusion | flops 761331712 | bytes 7405568 | tf_op jit(solution)/shard_map/conv_general_dilated | solution.py:28
  91.1 0.0 copy-done.3
  91.1 0.2 fusion.7
  91.3 0.9 copy.53
  (11 shorter events, 0.1 us)
Async XLA Ops:
  6.5 75.6 %copy-start = (bf16[2,2,2,512,256]{4,3,2,1,0:T(8,128)(2,1)S(1)}, bf16[2,2,2,512,256]{4,3,2,1,0:T(8,128)(2,1)}, u32[]{:S(2)}) copy-start(bf16[2,2,2,512,256]{4,3,2,1,0:T(8,128)(2,1)} %param.13) | copy-start | bytes 6291460
  6.5 76.4 %all-gather.2.cloned.1.call-start = ((), (), s32[]{:S(2)}) async-start(), calls=%async_computation | async-start | bytes 7520256 | tf_op jit(solution)/shard_map/all_gather | solution.py:270
  8.1 3.7 %collective-permute-start = (bf16[1,16,16,128]{3,2,1,0:T(8,128)(2,1)S(1)}, bf16[1,16,16,128]{3,2,1,0:T(8,128)(2,1)S(1)}, u32[]{:S(2)}, u32[]{:S(2)}) collective-permute-start(bf16[1,16,16,128]{3,2,1,0:T(8,128)(2,1)S(1)} %get-tuple-element.5), channel_id=1, source_target_pairs={{0,1},{1,2},{2,3},{3,4},{4,5},{5,6},{6,7},{7,8},{8,9},{9,10},{10,1... | collective-permute-start | bytes 196616 | tf_op jit(solution)/shard_map/ppermute | solution.py:17
  10.6 5.3 %collective-permute-start.1 = (bf16[1,16,16,128]{3,2,1,0:T(8,128)(2,1)S(1)}, bf16[1,16,16,128]{3,2,1,0:T(8,128)(2,1)S(1)}, u32[]{:S(2)}, u32[]{:S(2)}) collective-permute-start(bf16[1,16,16,128]{3,2,1,0:T(8,128)(2,1)S(1)} %get-tuple-element.6), channel_id=1, source_target_pairs={{1,0},{2,1},{3,2},{4,3},{5,4},{6,5},{7,6},{8,7},{9,8},{10,9},{11,1... | collective-permute-start | bytes 196616 | tf_op jit(solution)/shard_map/ppermute | solution.py:18
  16.8 14.6 %copy-start.2 = (bf16[3,3,3,512,32]{3,4,2,1,0:T(8,128)(2,1)S(1)}, bf16[3,3,3,512,32]{3,4,2,1,0:T(8,128)(2,1)}, u32[]{:S(2)}) copy-start(bf16[3,3,3,512,32]{3,4,2,1,0:T(8,128)(2,1)} %param.12) | copy-start | bytes 2654212
  25.2 15.1 %collective-permute-start.2 = (bf16[1,8,8,128]{3,2,1,0:T(8,128)(2,1)S(1)}, bf16[1,8,8,128]{3,2,1,0:T(8,128)(2,1)S(1)}, u32[]{:S(2)}, u32[]{:S(2)}) collective-permute-start(bf16[1,8,8,128]{3,2,1,0:T(8,128)(2,1)S(1)} %get-tuple-element.9), channel_id=1, source_target_pairs={{0,1},{1,2},{2,3},{3,4},{4,5},{5,6},{6,7},{7,8},{8,9},{9,10},{10,1... | collective-permute-start | bytes 49160 | tf_op jit(solution)/shard_map/ppermute | solution.py:17
  30.2 10.2 %collective-permute-start.3 = (bf16[1,8,8,128]{3,2,1,0:T(8,128)(2,1)S(1)}, bf16[1,8,8,128]{3,2,1,0:T(8,128)(2,1)S(1)}, u32[]{:S(2)}, u32[]{:S(2)}) collective-permute-start(bf16[1,8,8,128]{3,2,1,0:T(8,128)(2,1)S(1)} %get-tuple-element.10), channel_id=1, source_target_pairs={{1,0},{2,1},{3,2},{4,3},{5,4},{6,5},{7,6},{8,7},{9,8},{10,9},{11,1... | collective-permute-start | bytes 49160 | tf_op jit(solution)/shard_map/ppermute | solution.py:18
  38.0 1.3 %copy-start.1 = (bf16[9,256,96]{2,1,0:T(8,128)(2,1)S(1)}, bf16[9,256,96]{2,1,0:T(8,128)(2,1)}, u32[]{:S(2)}) copy-start(bf16[9,256,96]{2,1,0:T(8,128)(2,1)} %copy.47) | copy-start | bytes 1327108
  38.0 2.3 %copy-start.4 = (bf16[3,3,3,128,256]{4,3,2,1,0:T(8,128)(2,1)S(1)}, bf16[3,3,3,128,256]{4,3,2,1,0:T(8,128)(2,1)}, u32[]{:S(2)}) copy-start(bf16[3,3,3,128,256]{4,3,2,1,0:T(8,128)(2,1)} %param.10) | copy-start | bytes 5308420
  42.0 40.9 %collective-permute-start.4 = (bf16[1,8,8,256]{3,2,1,0:T(8,128)(2,1)S(1)}, bf16[1,8,8,256]{3,2,1,0:T(8,128)(2,1)S(1)}, u32[]{:S(2)}, u32[]{:S(2)}) collective-permute-start(bf16[1,8,8,256]{3,2,1,0:T(8,128)(2,1)S(1)} %bitcast.62), channel_id=1, source_target_pairs={{0,1},{1,2},{2,3},{3,4},{4,5},{5,6},{6,7},{7,8},{8,9},{9,10},{10,1... | collective-permute-start | bytes 98312 | tf_op jit(solution)/shard_map/ppermute | solution.py:17
  45.1 37.8 %collective-permute-start.5 = (bf16[1,8,8,256]{3,2,1,0:T(8,128)(2,1)S(1)}, bf16[1,8,8,256]{3,2,1,0:T(8,128)(2,1)S(1)}, u32[]{:S(2)}, u32[]{:S(2)}) collective-permute-start(bf16[1,8,8,256]{3,2,1,0:T(8,128)(2,1)S(1)} %bitcast.63), channel_id=1, source_target_pairs={{1,0},{2,1},{3,2},{4,3},{5,4},{6,5},{7,6},{8,7},{9,8},{10,9},{11,1... | collective-permute-start | bytes 98312 | tf_op jit(solution)/shard_map/ppermute | solution.py:18
  82.9 8.1 %copy-start.3 = (bf16[2,2,2,256,128]{4,3,2,1,0:T(8,128)(2,1)S(1)}, bf16[2,2,2,256,128]{4,3,2,1,0:T(8,128)(2,1)}, u32[]{:S(2)}) copy-start(bf16[2,2,2,256,128]{4,3,2,1,0:T(8,128)(2,1)} %param.15) | copy-start | bytes 1572868
Sparse Core Ops, SparseCore 0:
  9.5 73.0 all-gather.1

commit v2 on v1

--- a/solution.py
+++ b/solution.py
@@ -10,18 +10,149 @@
 LANES = 128
 
 
-def halo_slices(block, axis):
-    count = lax.axis_size(axis)
-    forward = [(i, i + 1) for i in range(count - 1)]
-    backward = [(target, source) for source, target in forward]
-    low = lax.ppermute(block[-1:], axis, forward)
-    high = lax.ppermute(block[:1], axis, backward)
-    return low, high
-
-
-def with_halo(block, axis):
-    low, high = halo_slices(block, axis)
-    return jnp.concatenate([low, block, high], axis=0)
+def remote(src, dst, send_sem, recv_sem, target):
+    return pltpu.make_async_remote_copy(
+        src_ref=src, dst_ref=dst, send_sem=send_sem, recv_sem=recv_sem,
+        device_id={"sp": target}, device_id_type=pl.DeviceIdType.MESH,
+    )
+
+
+def trade_edges(n, first, last, low, high, send_sem, recv_sem):
+    me = lax.axis_index("sp")
+    upward = remote(last, low, send_sem.at[0], recv_sem.at[0], lax.rem(me + 1, n))
+    downward = remote(first, high, send_sem.at[1], recv_sem.at[1], lax.rem(me + n - 1, n))
+
+    @pl.when(me < n - 1)
+    def _():
+        upward.start()
+
+    @pl.when(me > 0)
+    def _():
+        downward.start()
+
+    @pl.when(me == 0)
+    def _():
+        low[...] = jnp.zeros(low.shape, low.dtype)
+
+    @pl.when(me == n - 1)
+    def _():
+        high[...] = jnp.zeros(high.shape, high.dtype)
+
+    def finish():
+        @pl.when(me > 0)
+        def _():
+            upward.wait_recv()
+            downward.wait_send()
+
+        @pl.when(me < n - 1)
+        def _():
+            downward.wait_recv()
+            upward.wait_send()
+
+    return finish
+
+
+def greet_neighbours(n):
+    me = lax.axis_index("sp")
+    barrier = pltpu.get_barrier_semaphore()
+
+    @pl.when(me > 0)
+    def _():
+        pl.semaphore_signal(
+            barrier, inc=1, device_id={"sp": lax.rem(me + n - 1, n)},
+            device_id_type=pl.DeviceIdType.MESH,
+        )
+
+    @pl.when(me < n - 1)
+    def _():
+        pl.semaphore_signal(
+            barrier, inc=1, device_id={"sp": lax.rem(me + 1, n)},
+            device_id_type=pl.DeviceIdType.MESH,
+        )
+
+    @pl.when((me > 0) & (me < n - 1))
+    def _():
+        pl.semaphore_wait(barrier, 2)
+
+    @pl.when((me == 0) | (me == n - 1))
+    def _():
+        pl.semaphore_wait(barrier, 1)
+
+
+def first_level_kernel(
+    n, depth, height, width,
+    volume_ref, weight_ref, out_ref,
+    ends, taps, sums, send_a, recv_a, send_b, recv_b,
+):
+    area = height * width
+    chans = volume_ref.shape[2]
+    greet_neighbours(n)
+    finish = trade_edges(
+        n, volume_ref.at[0], volume_ref.at[depth - 1], ends.at[0], ends.at[1], send_a, recv_a
+    )
+    index = lax.broadcasted_iota(jnp.int32, (area, 1), 0) & (width - 1)
+    blank = jnp.zeros((depth + 2, width, 3 * chans), jnp.bfloat16)
+    taps[:, 0:width] = blank
+    taps[:, area + width : area + 2 * width] = blank
+
+    def spread(at, values):
+        taps[at, width : area + width, chans : 2 * chans] = values
+        values = values.astype(jnp.float32)
+        left = jnp.where(index > 0, pltpu.roll(values, 1, 0), 0.0)
+        right = jnp.where(index < width - 1, pltpu.roll(values, area - 1, 0), 0.0)
+        taps[at, width : area + width, 0:chans] = left.astype(jnp.bfloat16)
+        taps[at, width : area + width, 2 * chans : 3 * chans] = right.astype(jnp.bfloat16)
+
+    for d in range(depth):
+        spread(d + 1, volume_ref[d])
+    finish()
+    spread(0, ends[0])
+    spread(depth + 1, ends[1])
+    for pair in range(depth // 2):
+        total = jnp.zeros((2 * area, weight_ref.shape[3]), jnp.float32)
+        for a in range(3):
+            for b in range(3):
+                block = taps[2 * pair + a : 2 * pair + a + 2, b * width : b * width + area]
+                total += jnp.dot(
+                    block.reshape(2 * area, 3 * chans), weight_ref[a, b],
+                    preferred_element_type=jnp.float32,
+                )
+        total = jnp.maximum(total, 0.0).astype(jnp.bfloat16).astype(jnp.float32)
+        total = total[0:area] + total[area : 2 * area]
+        total = total.reshape(height // 2, 2, width, total.shape[1]).sum(axis=1)
+        sums[...] = total.reshape(area // 2, total.shape[2])
+        total = sums[pl.ds(0, area // 4, 2), :] + sums[pl.ds(1, area // 4, 2), :]
+        out_ref[1 + pair] = (total * 0.125).astype(jnp.bfloat16)
+    halves = depth // 2
+    trade_edges(
+        n, out_ref.at[1], out_ref.at[halves], out_ref.at[0], out_ref.at[halves + 1],
+        send_b, recv_b,
+    )()
+
+
+def first_level(volume, kernel):
+    n = lax.axis_size("sp")
+    depth, height, width, chans = volume.shape
+    outs = kernel.shape[4]
+    area = height * width
+    vmem = pl.BlockSpec(memory_space=pltpu.VMEM)
+    padded = pl.pallas_call(
+        functools.partial(first_level_kernel, n, depth, height, width),
+        out_shape=jax.ShapeDtypeStruct((depth // 2 + 2, area // 4, outs), jnp.bfloat16),
+        in_specs=[vmem] * 2,
+        out_specs=vmem,
+        scratch_shapes=[
+            pltpu.VMEM((2, area, chans), jnp.bfloat16),
+            pltpu.VMEM((depth + 2, area + 2 * width, 3 * chans), jnp.bfloat16),
+            pltpu.VMEM((area // 2, outs), jnp.float32),
+        ]
+        + [pltpu.SemaphoreType.DMA((2,))] * 4,
+        compiler_params=pltpu.CompilerParams(
+            collective_id=1, has_side_effects=True, vmem_limit_bytes=16 << 20
+        ),
+        name="first_level",
+    )(volume.reshape(depth, area, chans), kernel.reshape(3, 3, 3 * chans, outs))
+    return padded.reshape(depth // 2 + 2, height // 2, width // 2, outs)
 
 
 def conv_depth(padded, kernel):
@@ -53,6 +184,8 @@
     index = lax.broadcasted_iota(jnp.int32, (rows, 1), 0)
     w_at = index & (width - 1)
     h_at = (index >> (width.bit_length() - 1)) & (height - 1)
+    part, chans = weight_ref.shape[2:]
+    blank = jnp.zeros((LANES - 3 * part, chans), weight_ref.dtype)
     total = jnp.zeros((rows, LANES), jnp.float32)
     for b in range(3):
         for c in range(3):
@@ -61,15 +194,19 @@
             h_to, w_to = h_at + (b - 1), w_at + (c - 1)
             keep = (h_to >= 0) & (h_to < height) & (w_to >= 0) & (w_to < width)
             moved = jnp.where(keep, moved, 0.0).astype(jnp.bfloat16)
-            total += jnp.dot(moved, weight_ref[3 * b + c], preferred_element_type=jnp.float32)
+            tap = 3 * b + c
+            weight = jnp.concatenate([weight_ref[a, tap] for a in range(3)] + [blank], axis=0)
+            total += lax.dot_general(
+                moved, weight, (((1,), (1,)), ((), ())), preferred_element_type=jnp.float32
+            )
     return total
 
 
 def bottleneck_kernel(
     n, height, width, part,
-    pooled_ref, deep_w_ref, deeper_w_ref, out_ref,
+    pooled_ref, skip_ref, deep_w_ref, deeper_w_ref, out_ref, near_ref,
     whole, deep_mine, deep_all, packed,
-    send_a, recv_a, send_b, recv_b, send_c, recv_c,
+    send_a, recv_a, send_b, recv_b, send_c, recv_c, send_d, recv_d,
 ):
     me = lax.axis_index("sp")
     area = height * width
@@ -89,34 +226,28 @@
     lax.fori_loop(1, n, greet, 0)
     pl.semaphore_wait(barrier, n - 1)
 
-    def copy_to(src, dst, send_sem, recv_sem, target):
-        return pltpu.make_async_remote_copy(
-            src_ref=src, dst_ref=dst, send_sem=send_sem, recv_sem=recv_sem,
-            device_id={"sp": target}, device_id_type=pl.DeviceIdType.MESH,
-        )
-
     def gather(mine, everyone, send_sem, recv_sem):
         def slot(source):
             return everyone.at[source]
 
         def direct(k):
             target = lax.rem(me + 2 * k, n)
-            return copy_to(mine, slot(me), send_sem.at[k], recv_sem.at[me], target)
+            return remote(mine, slot(me), send_sem.at[k], recv_sem.at[me], target)
 
         def relay(k):
             source = lax.rem(me + 2 * (half - k), n)
-            return copy_to(
+            return remote(
                 slot(source), slot(source), send_sem.at[half + k], recv_sem.at[source], partner
             )
 
         def arrival(source):
-            return copy_to(mine, slot(source), send_sem.at[0], recv_sem.at[source], partner)
+            return remote(mine, slot(source), send_sem.at[0], recv_sem.at[source], partner)
 
         def start_direct(k, carry):
             direct(k).start()
             return carry
 
-        to_partner = copy_to(mine, slot(me), send_sem.at[0], recv_sem.at[me], partner)
+        to_partner = remote(mine, slot(me), send_sem.at[0], recv_sem.at[me], partner)
         lax.fori_loop(1, half, start_direct, 0)
         to_partner.start()
         everyone[me] = mine[...]
@@ -147,6 +278,10 @@
         return finish
 
     finish_a = gather(pooled_ref, whole, send_a, recv_a)
+    depth = skip_ref.shape[0]
+    finish_d = trade_edges(
+        n, skip_ref.at[0], skip_ref.at[depth - 1], near_ref.at[0], near_ref.at[1], send_d, recv_d
+    )
     lanes = lax.broadcasted_iota(jnp.int32, (1, voxels), 1)
     values = whole[...].astype(jnp.float32).reshape(voxels, pooled_ref.shape[1])
     deep = conv_rows(values, deep_w_ref, height, width).T
@@ -188,7 +323,7 @@
 
     def deal(k):
         target = lax.rem(me + k, n)
-        return copy_to(packed.at[target], out_ref.at[me], send_c.at[k], recv_c.at[me], target)
+        return remote(packed.at[target], out_ref.at[me], send_c.at[k], recv_c.at[me], target)
 
     def start_deal(k, carry):
         deal(k).start()
@@ -199,7 +334,7 @@
 
     def receive(k, carry):
         source = lax.rem(me + k, n)
-        copy_to(
+        remote(
             packed.at[source], out_ref.at[source], send_c.at[k], recv_c.at[source], source
         ).wait_recv()
         return carry
@@ -213,38 +348,44 @@
     lax.fori_loop(1, n, sent, 0)
     finish_a()
     finish_b()
-
-
-def stack_taps(kernel):
+    finish_d()
+
+
+def out_major(kernel):
     chans, part = kernel.shape[3], kernel.shape[4]
-    stacked = jnp.transpose(kernel, (1, 2, 3, 0, 4)).reshape(9, chans, 3 * part)
-    return jnp.pad(stacked, ((0, 0), (0, 0), (0, LANES - 3 * part)))
-
-
-def bottleneck(pooled, deep_kernel, deeper_kernel):
+    return jnp.transpose(kernel, (0, 1, 2, 4, 3)).reshape(3, 9, part, chans)
+
+
+def bottleneck(pooled, skip, deep_kernel, deeper_kernel):
     n = lax.axis_size("sp")
     _, height, width, chans = pooled.shape
     part = deep_kernel.shape[4]
     area = height * width
     voxels = n * area
     vmem = pl.BlockSpec(memory_space=pltpu.VMEM)
-    received = pl.pallas_call(
+    received, near = pl.pallas_call(
         functools.partial(bottleneck_kernel, n, height, width, part),
-        out_shape=jax.ShapeDtypeStruct((n, area, LANES), jnp.bfloat16),
-        in_specs=[vmem] * 3,
-        out_specs=vmem,
+        out_shape=(
+            jax.ShapeDtypeStruct((n, area, LANES), jnp.bfloat16),
+            jax.ShapeDtypeStruct((2,) + skip.shape[1:], jnp.bfloat16),
+        ),
+        in_specs=[vmem] * 4,
+        out_specs=(vmem, vmem),
         scratch_shapes=[
             pltpu.VMEM((n, area, chans), jnp.bfloat16),
             pltpu.VMEM((part, voxels), jnp.bfloat16),
             pltpu.VMEM((n, part, voxels), jnp.bfloat16),
             pltpu.VMEM((n, area, LANES), jnp.bfloat16),
         ]
-        + [pltpu.SemaphoreType.DMA((n,))] * 6,
-        compiler_params=pltpu.CompilerParams(collective_id=0, has_side_effects=True),
+        + [pltpu.SemaphoreType.DMA((n,))] * 6
+        + [pltpu.SemaphoreType.DMA((2,))] * 2,
+        compiler_params=pltpu.CompilerParams(
+            collective_id=0, has_side_effects=True, vmem_limit_bytes=24 << 20
+        ),
         name="bottleneck",
-    )(pooled.reshape(area, chans), stack_taps(deep_kernel), stack_taps(deeper_kernel))
+    )(pooled.reshape(area, chans), skip, out_major(deep_kernel), out_major(deeper_kernel))
     blocks = received[:, :, : 3 * part].reshape(n, area, 3, part)
-    return jnp.transpose(blocks, (2, 1, 0, 3)).reshape(3, height, width, n * part)
+    return jnp.transpose(blocks, (2, 1, 0, 3)).reshape(3, height, width, n * part), near
 
 
 def body(
@@ -257,14 +398,11 @@
     decode_kernel,
     final_kernel,
 ):
-    padded_input = with_halo(volume, "sp")
-    first = jax.nn.relu(conv_depth(padded_input, first_kernel)).astype(jnp.bfloat16)
-    pooled_one = pool_mean(first)
-    padded_pool = with_halo(pooled_one, "sp")
+    padded_pool = first_level(volume, first_kernel)
     skip = jax.nn.relu(conv_depth(padded_pool, second_kernel)).astype(jnp.bfloat16)
     pooled_two = pool_mean(skip)
-    padded_skip = with_halo(skip, "sp")
-    deeper_near = bottleneck(pooled_two, deep_kernel, deeper_kernel)
+    deeper_near, skip_near = bottleneck(pooled_two, skip, deep_kernel, deeper_kernel)
+    padded_skip = jnp.concatenate([skip_near[:1], skip, skip_near[1:]], axis=0)
     risen = up_conv(deeper_near, rise_kernel)[1:-1].astype(jnp.bfloat16)
     padded_joined = jnp.concatenate([risen, padded_skip], axis=3)
     whole_decode_kernel = lax.all_gather(decode_kernel, "sp", axis=3, tiled=True)

time: 99.6 us -> 98.3 us (0.987)
  waiting for transfers between devices: 4.7 us -> 30.5 us
  starting transfers between devices: 14.4 us -> 0.01 us
  local copies, waits for them, and re-layouts: 13.1 us -> 6.47 us
  matrix products: 16.9 us -> 11.6 us
  other arithmetic: 2.88 us -> 1.02 us
  Pallas kernels: 33.5 us -> 34.8 us
    all_gather x1, waiting for transfers between devices: 0.02 us -> 29.8 us  [body(): lax.all_gather(decode_kernel, 'sp', axis=3, tiled=True)]
    ppermute x6 -> x0, starting transfers between devices: 14.4 us -> none  [the longest x3 10.4 us: halo_slices(): low = lax.ppermute(block[-1:], axis, forward)]
    pallas_call x0 -> x1, Pallas kernels: none -> 7.84 us  [first_level(): pl.pallas_call(functools.partial(first_level_kernel, n, depth, height, wi...]
    pallas_call x1, Pallas kernels: 33.5 us -> 26.9 us  [bottleneck(): pl.pallas_call(functools.partial(bottleneck_kernel, n, height, width, par...]
    conv_general_dilated x3 -> x2, matrix products: 16.2 us -> 10.9 us  [conv_depth(): lax.conv_general_dilated(padded[None], kernel, (1, 1, 1), ((0, 0), (1, 1)...]
    ppermute x6 -> x0, waiting for transfers between devices: 3.97 us -> none  [the longest x3 3.96 us: halo_slices(): high = lax.ppermute(block[:1], axis, backward)]
    reshape x2 -> x0, local copies, waits for them, and re-layouts: 3.77 us -> none  [stack_taps(): stacked = jnp.transpose(kernel, (1, 2, 3, 0, 4)).reshape(9, chans, 3 * part)]
    pad x2 -> x0, local copies, waits for them, and re-layouts: 2.28 us -> none  [stack_taps(): return jnp.pad(stacked, ((0, 0), (0, 0), (0, LANES - 3 * part)))]
  transfers between devices with their start and end apart: 7 -> 1, of which waited for: 1 -> 1; matrix products, arithmetic and copies ran while one was open for 24% -> 6% of each run, Pallas kernels for 34% -> 36%
where the time goes in v2:
time: 98.3 us; the launch traced here: 97.9 us
  Pallas kernels  34.8 us (35%)
  waiting for transfers between devices  30.5 us (31%)
  between operations  13.6 us (14%)
  matrix products  11.6 us (12%)
  local copies, waits for them, and re-layouts  6.47 us (7%)
  other arithmetic  1.02 us (1%)
    all_gather x1, waiting for transfers between devices, body(): lax.all_gather(decode_kernel, 'sp', axis=3, tiled=True)  29.8 us
    pallas_call x1, Pallas kernels, bottleneck(): pl.pallas_call(functools.partial(bottleneck_kernel, n, height, width, par...  26.9 us
    conv_general_dilated x2, matrix products, conv_depth(): lax.conv_general_dilated(padded[None], kernel, (1, 1, 1), ((0, 0), (1, 1)...  10.9 us
    pallas_call x1, Pallas kernels, first_level(): pl.pallas_call(functools.partial(first_level_kernel, n, depth, height, wi...  7.84 us
    unnamed x20, local copies, waits for them, and re-layouts  4.18 us
  transfers between devices with their start and end apart: 1, of which 1 were waited for; matrix products, arithmetic and copies ran while one was open for 6% of the time, Pallas kernels for 36%

profile of v2, /device:TPU:0, one launch (start us, length us, event | category | flops | bytes accessed | tf_op | source)
XLA Modules:
  0.0 97.9 jit_solution(3923902747887136375)
XLA Ops:
  6.5 0.0 copy-start
  6.5 0.0 all-gather.2.cloned.1.call-start
  6.5 0.7 all-gather.2.cloned.1.call-update
  7.3 0.0 copy-start.1
  7.3 1.2 %copy-done.1 = bf16[3,3,3,128,128]{4,3,2,1,0:T(8,128)(2,1)S(1)} copy-done((bf16[3,3,3,128,128]{4,3,2,1,0:T(8,128)(2,1)S(1)}, bf16[3,3,3,128,128]{4,3,2,1,0:T(8,128)(2,1)}, u32[]{:S(2)}) %copy-start.1) | copy-done | bytes 884760
  8.4 0.0 copy-start.4
  8.4 0.9 copy-done.4
  9.4 7.8 %first_level.1 = bf16[4,64,128]{2,1,0:T(8,128)(2,1)S(1)} custom-call(bf16[4,256,128]{2,1,0:T(8,128)(2,1)S(1)} %bitcast.51, bf16[3,3,384,128]{3,2,1,0:T(8,128)(2,1)S(1)} %bitcast.48), custom_call_target="tpu_custom_call" | custom-call | tf_op jit(solution)/shard_map/first_level/pallas_call | solution.py:139
  17.2 0.0 copy-start.2
  17.2 0.0 copy-start.3
  17.2 2.8 %fusion.14 = bf16[1,2,8,8,256]{4,0,3,2,1:T(2,128)(2,1)S(1)} fusion(bf16[3,3,3,128,256]{4,3,2,1,0:T(8,128)(2,1)} %param.10, bf16[1,4,8,8,128]{4,3,2,1,0:T(8,128)(2,1)S(1)} %bitcast.53), kind=kOutput, calls=%fused_computation.14 | convolution fusion | flops 190316544 | bytes 1900544 | tf_op jit(solution)/shard_map/conv_general_dilated | solution.py:159
  20.1 0.0 copy-start.8
  20.1 0.6 copy-done.8
  20.8 0.1 reduce_sum.18
  20.9 0.6 convert_element_type.38.pooled_ref
  21.5 0.9 fusion.20.skip_ref
  22.4 0.0 copy-done.2
  22.4 0.0 copy-done.3
  22.4 0.0 copy-start.7
  22.4 0.7 copy-done.7
  23.1 26.9 %bottleneck.1 = (bf16[16,16,128]{2,1,0:T(8,128)(2,1)S(1)}, bf16[2,8,8,256]{3,2,1,0:T(8,128)(2,1)S(1)}) custom-call(bf16[16,256]{1,0:T(8,128)(2,1)S(1)} %copy-done.7, bf16[2,8,8,256]{3,2,1,0:T(8,128)(2,1)S(1)} %fusion.20.skip_ref, bf16[3,9,32,256]{3,2,1,0:T(8,128)(2,1)S(1)} %bitcast.50, bf16[3,9,32,512]{3,2,1,0:T(8,128)(2,1)S(1)} %bitcast.49), custom_call_target="tpu_custom_call" | custom-call | tf_op jit(solution)/shard_map/bottleneck/pallas_call | solution.py:366
  50.1 0.0 copy-start.5
  50.1 0.6 copy-done.5
  50.7 0.1 reshape.49
  50.8 0.2 copy.32
  51.0 0.2 reshape.52
  51.2 0.0 copy-done
  51.2 0.0 copy-start.6
  51.2 0.5 fusion.6
  51.7 0.2 copy.33
  51.9 0.1 reshape.51
  52.0 0.1 copy-done.6
  52.1 0.0 copy-start.9
  52.1 29.8 %all-gather.2.cloned.1.call-done = bf16[3,3,3,512,256]{4,3,2,1,0:T(8,128)(2,1)} async-done(((bf16[3,3,3,32,256]{4,3,2,1,0:T(8,128)(2,1)}), bf16[3,3,3,512,256]{4,3,2,1,0:T(8,128)(2,1)}) %all-gather.2.cloned.1.call-update) | async-done | bytes 7077904 | tf_op jit(solution)/shard_map/all_gather | solution.py:408
  81.9 8.0 %fusion.10 = bf16[1,2,8,8,256]{4,0,3,2,1:T(2,128)(2,1)S(1)} fusion(bf16[3,3,3,512,256]{4,3,2,1,0:T(8,128)(2,1)} %all-gather.2.cloned.1.call-done, bf16[1,4,8,8,512]{4,3,2,1,0:T(8,128)(2,1)S(1)} %maximum_bitcast_fusion), kind=kOutput, calls=%fused_computation.7 | convolution fusion | flops 761266176 | bytes 7405568 | tf_op jit(solution)/shard_map/conv_general_dilated | solution.py:159
  89.9 0.0 copy-done.9
  89.9 0.2 fusion.5
  90.2 0.9 copy.36
  (6 shorter events, 0.1 us)
Async XLA Ops:
  6.5 44.7 %copy-start = (bf16[2,2,2,512,256]{4,3,2,1,0:T(8,128)(2,1)S(1)}, bf16[2,2,2,512,256]{4,3,2,1,0:T(8,128)(2,1)}, u32[]{:S(2)}) copy-start(bf16[2,2,2,512,256]{4,3,2,1,0:T(8,128)(2,1)} %param.13) | copy-start | bytes 6291460
  6.5 75.3 %all-gather.2.cloned.1.call-start = ((), (), s32[]{:S(2)}) async-start(), calls=%async_computation | async-start | bytes 7520256 | tf_op jit(solution)/shard_map/all_gather | solution.py:408
  7.3 1.2 %copy-start.1 = (bf16[3,3,3,128,128]{4,3,2,1,0:T(8,128)(2,1)S(1)}, bf16[3,3,3,128,128]{4,3,2,1,0:T(8,128)(2,1)}, u32[]{:S(2)}) copy-start(bf16[3,3,3,128,128]{4,3,2,1,0:T(8,128)(2,1)} %param.9) | copy-start | bytes 2654212
  8.4 0.9 copy-start.4
  17.2 5.2 %copy-start.2 = (bf16[3,3,3,512,32]{3,4,2,1,0:T(8,128)(2,1)S(1)}, bf16[3,3,3,512,32]{3,4,2,1,0:T(8,128)(2,1)}, u32[]{:S(2)}) copy-start(bf16[3,3,3,512,32]{3,4,2,1,0:T(8,128)(2,1)} %param.12) | copy-start | bytes 2654212
  17.2 5.2 %copy-start.3 = (bf16[3,3,3,256,32]{3,4,2,1,0:T(8,128)(2,1)S(1)}, bf16[3,3,3,256,32]{3,4,2,1,0:T(8,128)(2,1)}, u32[]{:S(2)}) copy-start(bf16[3,3,3,256,32]{3,4,2,1,0:T(8,128)(2,1)} %param.11) | copy-start | bytes 1327108
  20.1 0.7 copy-start.8
  22.4 0.7 copy-start.7
  50.1 0.6 copy-start.5
  51.2 0.8 copy-start.6
  52.1 37.8 %copy-start.9 = (bf16[2,2,2,256,128]{4,3,2,1,0:T(8,128)(2,1)S(1)}, bf16[2,2,2,256,128]{4,3,2,1,0:T(8,128)(2,1)}, u32[]{:S(2)}) copy-start(bf16[2,2,2,256,128]{4,3,2,1,0:T(8,128)(2,1)} %param.15) | copy-start | bytes 1572868
Sparse Core Ops, SparseCore 0:
  9.5 72.3 all-gather.1
